TPU v7x, 32 devices: a whole 2x2x4 slice. The times are simulated.
32 devices in a mesh: band: 16 (over z, y, x), mem: 2 (over core).
Axes of the slice: x: 2, y: 2, z: 4, core: 2. Of those that a mesh axis runs over, the one named last changes fastest.
Arguments:
- state: float32 [16384, 2048], P('band', 'mem'), may hold values from -10 to 10
- obs_anom: bfloat16 [4096, 2048], P('band', 'mem'), may hold values from -8 to 8
- innov: float32 [4096, 2048], P('band', 'mem'), may hold values from -12 to 12
- pattern: int32 [16, 4, 8, 4], P('band'), may hold values 0 or 1
- distance: int32 [16, 4, 8, 4], P('band'), may hold values from 0 to 7
- taper: float32 [8], replicated, may hold values from 0.2 to 1
- order: int32 [16, 4], P('band'), may hold values from 0 to 3, each once within a row
Outputs:
- analysis: float32 [16384, 2048], P('band', 'mem')
Inputs may be any that keep to these rules, and one draw needn't show every extreme that they name: Each row of order lists 0 .. 3 once each.
All inputs are finite; a program needn't handle non-finite values. No bound on the sum of `pattern` on one device may be relied on, other than what follows from the above.
Results may differ from a plain program's by a relative error of at most 0.0028.
Values may be sent and summed in bfloat16 or wider, within the bound.
A program may use at most 64 MiB of HBM per device.

v0:
```python
import jax
import jax.numpy as jnp
from jax import lax
from jax.sharding import PartitionSpec as P


def from_behind(value, axis, steps):
    count = lax.axis_size(axis)
    pairs = [(source, (source + steps) % count) for source in range(count)]
    return lax.ppermute(value, axis, pairs)


def spread(blocks):
    rows, cols = blocks.shape
    return jnp.broadcast_to(blocks[:, None, :, None], (rows, 128, cols, 64)).reshape(
        rows * 128, cols * 64
    )


def on_device(state, obs_anom, innov, pattern, distance, taper, order):
    members = lax.axis_size("mem") * state.shape[1]
    scale = 1.0 / (members - 1)
    num_obs = obs_anom.shape[0]
    arrivals = order.shape[1]
    gram_part = jnp.dot(obs_anom, obs_anom.T, preferred_element_type=jnp.float32)
    gram = lax.psum(gram_part, "mem")
    spd = gram * scale + jnp.eye(num_obs, dtype=jnp.float32)
    factor = jnp.linalg.cholesky(spd)
    weights_own = jax.scipy.linalg.cho_solve((factor, True), innov).astype(jnp.bfloat16)
    own_batch = jnp.stack([obs_anom, weights_own])
    batches = [own_batch]
    current = own_batch
    for offset in range(1, arrivals):
        current = from_behind(current, "band", 1)
        batches.append(current)
    stacked = jnp.stack(batches)
    onehot = (distance[0][..., None] == jnp.arange(taper.shape[0], dtype=jnp.int32)).astype(
        jnp.float32
    )
    local = pattern[0].astype(jnp.float32) * jnp.sum(onehot * taper, axis=-1)
    field = state
    for step in range(arrivals):
        offset = order[0, step]
        chosen = lax.dynamic_index_in_dim(stacked, offset, 0, keepdims=False)
        y_batch = chosen[0].astype(jnp.float32)
        w_batch = chosen[1].astype(jnp.float32)
        blocks = lax.dynamic_index_in_dim(local, offset, 0, keepdims=False)
        cross_part = jnp.dot(field, y_batch.T, precision=lax.Precision.HIGHEST)
        cross = lax.psum(cross_part, "mem")
        field = field + jnp.dot(
            cross * scale * spread(blocks), w_batch, precision=lax.Precision.HIGHEST
        )
    return field


def solution(mesh):
    return jax.shard_map(
        on_device,
        mesh=mesh,
        in_specs=(
            P("band", "mem"),
            P("band", "mem"),
            P("band", "mem"),
            P("band", None, None, None),
            P("band", None, None, None),
            P(),
            P("band", None),
        ),
        out_specs=P("band", "mem"),
        check_vma=False,
    )
```

profile of v0, /device:TPU:0, one launch (start us, length us, event | category | flops | bytes accessed | tf_op | source)
XLA Modules:
  0.0 313.7 jit_solution(5123660919342085485)
XLA Ops:
  6.5 2.3 fusion.45
  8.9 0.0 all-reduce.7.cloned.1.call-update
  8.9 0.0 all-reduce.9.cloned.1.call-start
  9.0 21.7 %all-reduce.7.cloned.1.call-done = f32[256,256]{0,1:T(8,128)} async-done(((f32[256,256]{0,1:T(8,128)}), f32[256,256]{0,1:T(8,128)}) %all-reduce.7.cloned.1.call-update) | async-done | bytes 262160 | tf_op jit(solution)/shard_map/psum | solution.py:26
  30.6 1.0 convert_add_fusion
  31.6 0.1 copy.12
  31.8 1.0 fusion.18
  32.8 11.7 %cholesky.50 = f32[128,128]{1,0:T(8,128)S(1)} custom-call(f32[128,128]{1,0:T(8,128)S(1)} %cholesky.118), custom_call_target="Cholesky" | custom-call | tf_op jit(solution)/shard_map/jit(cholesky)/cholesky | solution.py:28
  44.5 9.8 %custom-call.18 = f32[1,128,128]{1,2,0:T(8,128)S(1)} custom-call(f32[1,128,128]{2,1,0:T(8,128)S(1)} %get-tuple-element.28), custom_call_target="InvertDiagBlocksLowerTriangular" | custom-call | tf_op jit(solution)/shard_map/jit(cholesky)/cholesky | solution.py:28
  54.4 0.2 constant_dynamic-update-slice_fusion
  54.6 0.3 convolution_subtract_fusion.2
  54.9 11.7 %cholesky.105 = f32[128,128]{1,0:T(8,128)S(1)} custom-call(f32[128,128]{1,0:T(8,128)S(1)} %convolution_subtract_fusion.2), custom_call_target="Cholesky" | custom-call | tf_op jit(solution)/shard_map/jit(cholesky)/cholesky | solution.py:28
  66.6 0.7 compare_reduce_fusion
  68.7 0.1 triangular_solve.73
  68.8 4.2 %while.1 = (s32[]{:T(128)}, f32[256,256]{1,0:T(8,128)S(1)}, s32[2,2]{1,0:T(2,128)S(1)}, f32[2,128,128]{2,1,0:T(8,128)S(1)}, s32[]{:T(128)}) while((s32[]{:T(128)}, f32[256,256]{1,0:T(8,128)S(1)}, s32[2,2]{1,0:T(2,128)S(1)}, f32[2,128,128]{2,1,0:T(8,128)S(1)}, s32[]{:T(128)}) %tuple.30), condition=%wide.while_cond, body=%wide.while_body.sunk | while | flops 2 | bytes 131181 | solution.py:29
  68.9 0.6 fusion.60
  69.5 1.4 bitcast_dynamic-update-slice_fusion.2
  70.9 0.6 fusion.60
  71.5 1.4 bitcast_dynamic-update-slice_fusion.2
  73.0 0.0 copy-start.5
  73.0 19.7 %custom-call.19 = f32[2,128,128]{1,2,0:T(8,128)S(1)} custom-call(f32[2,128,128]{2,1,0:T(8,128)S(1)} %get-tuple-element.12), custom_call_target="InvertDiagBlocksLowerTriangular" | custom-call | tf_op jit(solution)/shard_map/jit(_cho_solve)/triangular_solve | solution.py:29
  92.7 0.6 fusion.16
  93.3 0.6 convolution_subtract_fusion.1
  93.9 0.6 fusion.23
  94.5 0.6 fusion.22
  95.1 0.6 convolution_subtract_fusion
  95.8 0.6 fusion
  96.4 0.2 fusion.42
  96.6 1.8 collective-permute-start
  98.4 27.3 %collective-permute-done = bf16[2,256,1024]{2,1,0:T(8,128)(2,1)S(1)} collective-permute-done((bf16[2,256,1024]{2,1,0:T(8,128)(2,1)S(1)}, bf16[2,256,1024]{2,1,0:T(8,128)(2,1)S(1)}, u32[]{:S(2)}, u32[]{:S(2)}) %collective-permute-start) | collective-permute-done | bytes 1048608 | tf_op jit(solution)/shard_map/ppermute | solution.py:10
  125.7 28.3 %collective-permute-done.1 = bf16[2,256,1024]{2,1,0:T(8,128)(2,1)} collective-permute-done((bf16[2,256,1024]{2,1,0:T(8,128)(2,1)S(1)}, bf16[2,256,1024]{2,1,0:T(8,128)(2,1)}, u32[]{:S(2)}, u32[]{:S(2)}) %collective-permute-start.1) | collective-permute-done | bytes 1048608 | tf_op jit(solution)/shard_map/ppermute | solution.py:10
  153.9 0.7 fusion.44
  156.6 25.0 %collective-permute-done.2 = bf16[2,256,1024]{2,1,0:T(8,128)(2,1)} collective-permute-done((bf16[2,256,1024]{2,1,0:T(8,128)(2,1)}, bf16[2,256,1024]{2,1,0:T(8,128)(2,1)}, u32[]{:S(2)}, u32[]{:S(2)}) %collective-permute-start.2) | collective-permute-done | bytes 1048608 | tf_op jit(solution)/shard_map/ppermute | solution.py:10
  181.6 1.9 pad_maximum_fusion
  183.5 1.9 copy-done.3
  185.5 3.2 %convolution_bitcast_fusion = f32[1024,256]{0,1:T(8,128)} fusion(f32[1024,1024]{1,0:T(8,128)S(1)} %copy-done.4, bf16[4,2,256,1024]{3,2,1,0:T(8,128)(2,1)S(1)} %pad_maximum_fusion, s32[]{:T(128)S(6)} %select_n.23), kind=kOutput, calls=%fused_computation.7 | convolution fusion | flops 3221225472 | bytes 5767172 | tf_op jit(solution)/shard_map/dot_general | solution.py:48
  188.6 0.0 all-reduce.9.cloned.1.call-update
  188.6 0.3 all-reduce.11.cloned.1.call-start
  194.7 0.2 select_reduce_fusion
  195.0 9.1 %all-reduce.9.cloned.1.call-done = f32[1024,256]{0,1:T(8,128)} async-done(((f32[1024,256]{0,1:T(8,128)}), f32[1024,256]{0,1:T(8,128)}) %all-reduce.9.cloned.1.call-update) | async-done | bytes 1048592 | tf_op jit(solution)/shard_map/psum | solution.py:49
  204.1 0.1 broadcast_in_dim.19
  204.2 4.9 %convolution_add_fusion.3 = f32[1024,1024]{1,0:T(8,128)S(1)} fusion(f32[1024,1024]{1,0:T(8,128)} %param.7, f32[32,8,8,128]{3,2,1,0:T(8,128)S(1)} %bitcast.125, f32[1024,256]{0,1:T(8,128)} %all-reduce.9.cloned.1.call-done, bf16[4,2,256,1024]{3,2,1,0:T(8,128)(2,1)} %copy-done.3, s32[]{:T(128)S(6)} %select_n.23, s32[]{:T(128)S(6)} %add.80), kind=kOutput, calls=%fused_computation.6 | convolution fusion | flops 3222798336 | bytes 11010056 | tf_op jit(solution)/shard_map/dot_general | solution.py:50
  209.1 0.0 copy-start.2
  209.1 2.0 copy-done.2
  211.1 4.2 %fusion.11 = f32[1024,256]{0,1:T(8,128)} fusion(f32[1024,1024]{1,0:T(8,128)S(1)} %convolution_add_fusion.3, bf16[4,2,256,1024]{3,2,1,0:T(8,128)(2,1)} %copy-done.3, s32[]{:T(128)S(6)} %select_n.24), kind=kOutput, calls=%fused_computation.34 | convolution fusion | flops 3221225472 | bytes 5767172 | tf_op jit(solution)/shard_map/dot_general | solution.py:48
  215.4 0.0 all-reduce.11.cloned.1.call-update
  215.4 0.0 all-reduce.13.cloned.1.call-start
  215.5 20.7 %all-reduce.11.cloned.1.call-done = f32[1024,256]{0,1:T(8,128)} async-done(((f32[1024,256]{0,1:T(8,128)}), f32[1024,256]{0,1:T(8,128)}) %all-reduce.11.cloned.1.call-update) | async-done | bytes 1048592 | tf_op jit(solution)/shard_map/psum | solution.py:49
  236.2 0.1 broadcast_in_dim.39
  236.3 4.9 %convolution_add_fusion.2 = f32[1024,1024]{1,0:T(8,128)S(1)} fusion(f32[1024,1024]{1,0:T(8,128)} %copy-done.2, f32[32,8,8,128]{3,2,1,0:T(8,128)S(1)} %bitcast.123, f32[1024,256]{0,1:T(8,128)} %all-reduce.11.cloned.1.call-done, bf16[4,2,256,1024]{3,2,1,0:T(8,128)(2,1)} %copy-done.3, s32[]{:T(128)S(6)} %select_n.24, s32[]{:T(128)S(6)} %add.80), kind=kOutput, calls=%fused_computation.5 | convolution fusion | flops 3222798336 | bytes 11010056 | tf_op jit(solution)/shard_map/dot_general | solution.py:50
  241.2 0.0 copy-start.1
  241.2 2.0 copy-done.1
  243.2 4.2 %fusion.10 = f32[1024,256]{0,1:T(8,128)} fusion(f32[1024,1024]{1,0:T(8,128)S(1)} %convolution_add_fusion.2, bf16[4,2,256,1024]{3,2,1,0:T(8,128)(2,1)} %copy-done.3, s32[]{:T(128)S(6)} %select_n.25), kind=kOutput, calls=%fused_computation.31 | convolution fusion | flops 3221225472 | bytes 5767172 | tf_op jit(solution)/shard_map/dot_general | solution.py:48
  247.5 0.0 all-reduce.13.cloned.1.call-update
  247.5 0.3 all-reduce.15.cloned.1.call-start
  247.8 20.5 %all-reduce.13.cloned.1.call-done = f32[1024,256]{0,1:T(8,128)} async-done(((f32[1024,256]{0,1:T(8,128)}), f32[1024,256]{0,1:T(8,128)}) %all-reduce.13.cloned.1.call-update) | async-done | bytes 1048592 | tf_op jit(solution)/shard_map/psum | solution.py:49
  268.3 0.1 broadcast_in_dim.41
  268.4 4.9 %convolution_add_fusion.1 = f32[1024,1024]{1,0:T(8,128)S(1)} fusion(f32[1024,1024]{1,0:T(8,128)} %copy-done.1, f32[32,8,8,128]{3,2,1,0:T(8,128)S(1)} %bitcast.124, f32[1024,256]{0,1:T(8,128)} %all-reduce.13.cloned.1.call-done, bf16[4,2,256,1024]{3,2,1,0:T(8,128)(2,1)} %copy-done.3, s32[]{:T(128)S(6)} %select_n.25, s32[]{:T(128)S(6)} %add.80), kind=kOutput, calls=%fused_computation.4 | convolution fusion | flops 3222798336 | bytes 11010056 | tf_op jit(solution)/shard_map/dot_general | solution.py:50
  273.3 2.0 copy-done
  275.3 4.3 %fusion.9 = f32[1024,256]{0,1:T(8,128)} fusion(f32[1024,1024]{1,0:T(8,128)S(1)} %convolution_add_fusion.1, bf16[4,2,256,1024]{3,2,1,0:T(8,128)(2,1)} %copy-done.3, s32[]{:T(128)S(6)} %select_n.26), kind=kOutput, calls=%fused_computation.28 | convolution fusion | flops 3221225472 | bytes 5767172 | tf_op jit(solution)/shard_map/dot_general | solution.py:48
  279.6 0.0 all-reduce.15.cloned.1.call-update
  279.6 20.8 %all-reduce.15.cloned.1.call-done = f32[1024,256]{0,1:T(8,128)} async-done(((f32[1024,256]{0,1:T(8,128)}), f32[1024,256]{0,1:T(8,128)}) %all-reduce.15.cloned.1.call-update) | async-done | bytes 1048592 | tf_op jit(solution)/shard_map/psum | solution.py:49
  300.3 0.1 broadcast_in_dim.43
  300.5 6.7 %convolution_add_fusion = f32[1024,1024]{1,0:T(8,128)} fusion(f32[1024,1024]{1,0:T(8,128)} %copy-done, f32[32,8,8,128]{3,2,1,0:T(8,128)S(1)} %bitcast.122, f32[1024,256]{0,1:T(8,128)} %all-reduce.15.cloned.1.call-done, bf16[4,2,256,1024]{3,2,1,0:T(8,128)(2,1)} %copy-done.3, s32[]{:T(128)S(6)} %select_n.26, s32[]{:T(128)S(6)} %add.80), kind=kOutput, calls=%fused_computation.3 | convolution fusion | flops 3222798336 | bytes 11010056 | tf_op jit(solution)/shard_map/dot_general | solution.py:50
  (30 shorter events, 0.2 us)
Async XLA Ops:
  6.5 86.1 %copy-start.6 = (f32[256,1024]{1,0:T(8,128)S(1)}, f32[256,1024]{1,0:T(8,128)}, u32[]{:S(2)}) copy-start(f32[256,1024]{1,0:T(8,128)} %param.9) | copy-start | bytes 3145732
  6.5 24.1 %all-reduce.7.cloned.1.call-start = ((), (), s32[]{:S(2)}) async-start(), calls=%async_computation | async-start | bytes 524288 | tf_op jit(solution)/shard_map/psum | solution.py:26
  8.9 195.2 %all-reduce.9.cloned.1.call-start = ((), (), s32[]{:S(2)}) async-start(), calls=%async_computation.1 | async-start | bytes 2097152 | tf_op jit(solution)/shard_map/psum | solution.py:49
  73.0 23.4 %copy-start.5 = (bf16[256,1024]{1,0:T(8,128)(2,1)S(1)}, bf16[256,1024]{1,0:T(8,128)(2,1)}, u32[]{:S(2)}) copy-start(bf16[256,1024]{1,0:T(8,128)(2,1)} %param.8) | copy-start | bytes 1572868
  93.9 60.0 %copy-start.9 = (s32[1,4]{1,0:T(1,128)S(1)}, s32[1,4]{1,0:T(1,128)}, u32[]{:S(2)}) copy-start(s32[1,4]{1,0:T(1,128)} %param.13) | copy-start | bytes 52
  96.6 29.1 %collective-permute-start = (bf16[2,256,1024]{2,1,0:T(8,128)(2,1)S(1)}, bf16[2,256,1024]{2,1,0:T(8,128)(2,1)S(1)}, u32[]{:S(2)}, u32[]{:S(2)}) collective-permute-start(bf16[2,256,1024]{2,1,0:T(8,128)(2,1)S(1)} %get-tuple-element.24), channel_id=1, source_target_pairs={{0,2},{2,4},{4,6},{6,8},{8,10},{10,12},{12,14},{14,16},{16,18},{18... | collective-permute-start | bytes 3145736 | tf_op jit(solution)/shard_map/ppermute | solution.py:10
  125.7 28.3 %collective-permute-start.1 = (bf16[2,256,1024]{2,1,0:T(8,128)(2,1)S(1)}, bf16[2,256,1024]{2,1,0:T(8,128)(2,1)}, u32[]{:S(2)}, u32[]{:S(2)}) collective-permute-start(bf16[2,256,1024]{2,1,0:T(8,128)(2,1)S(1)} %collective-permute-done), channel_id=1, source_target_pairs={{0,2},{2,4},{4,6},{6,8},{8,10},{10,12},{12,14},{14,16},{16,18},{18... | collective-permute-start | bytes 3145736 | tf_op jit(solution)/shard_map/ppermute | solution.py:10
  153.9 27.6 %collective-permute-start.2 = (bf16[2,256,1024]{2,1,0:T(8,128)(2,1)}, bf16[2,256,1024]{2,1,0:T(8,128)(2,1)}, u32[]{:S(2)}, u32[]{:S(2)}) collective-permute-start(bf16[2,256,1024]{2,1,0:T(8,128)(2,1)} %collective-permute-done.1), channel_id=1, source_target_pairs={{0,2},{2,4},{4,6},{6,8},{8,10},{10,12},{12,14},{14,16},{16,18},{18... | collective-permute-start | bytes 3145736 | tf_op jit(solution)/shard_map/ppermute | solution.py:10
  181.6 3.9 %copy-start.4 = (f32[1024,1024]{1,0:T(8,128)S(1)}, f32[1024,1024]{1,0:T(8,128)}, u32[]{:S(2)}) copy-start(f32[1024,1024]{1,0:T(8,128)} %param.7) | copy-start | bytes 12582916
  183.5 1.9 copy-start.3
  185.4 9.3 %copy-start.8 = (s32[1,4,8,4]{2,3,1,0:T(4,128)S(1)}, s32[1,4,8,4]{2,3,1,0:T(4,128)}, u32[]{:S(2)}) copy-start(s32[1,4,8,4]{2,3,1,0:T(4,128)} %param.11) | copy-start | bytes 1540
  185.4 9.3 %copy-start.10 = (f32[8]{0:T(128)S(1)}, f32[8]{0:T(128)}, u32[]{:S(2)}) copy-start(f32[8]{0:T(128)} %param.12) | copy-start | bytes 100
  185.5 9.5 %copy-start.7 = (s32[1,4,8,4]{2,3,1,0:T(4,128)S(1)}, s32[1,4,8,4]{2,3,1,0:T(4,128)}, u32[]{:S(2)}) copy-start(s32[1,4,8,4]{2,3,1,0:T(4,128)} %param.10) | copy-start | bytes 1540
  188.6 47.5 %all-reduce.11.cloned.1.call-start = ((), (), s32[]{:S(2)}) async-start(), calls=%async_computation.2 | async-start | bytes 2097152 | tf_op jit(solution)/shard_map/psum | solution.py:49
  209.1 2.0 copy-start.2
  215.4 52.9 %all-reduce.13.cloned.1.call-start = ((), (), s32[]{:S(2)}) async-start(), calls=%async_computation.3 | async-start | bytes 2097152 | tf_op jit(solution)/shard_map/psum | solution.py:49
  241.2 2.0 copy-start.1
  247.5 52.9 %all-reduce.15.cloned.1.call-start = ((), (), s32[]{:S(2)}) async-start(), calls=%async_computation.4 | async-start | bytes 2097152 | tf_op jit(solution)/shard_map/psum | solution.py:49
  273.3 2.0 copy-start
Sparse Core Ops, SparseCore 0:
  9.7 20.9 all-reduce.6
  188.8 15.2 all-reduce.8
  215.5 20.5 all-reduce.10
  247.6 20.6 all-reduce.12
  279.7 20.5 all-reduce.14
where the time goes:
time: 314 us
  waiting for transfers between devices  173 us (55%)
  other arithmetic  58 us (18%)
  matrix products  43.7 us (14%)
  between operations  22.5 us (7%)
  local copies, waits for them, and re-layouts  13.5 us (4%)
    ppermute x3, waiting for transfers between devices, from_behind(): return lax.ppermute(value, axis, pairs)  80.5 us
    psum x4, waiting for transfers between devices, on_device(): cross = lax.psum(cross_part, 'mem')  71 us
    another operation x6, other arithmetic, on_device(): factor = jnp.linalg.cholesky(spd)  34 us
    psum x1, waiting for transfers between devices, on_device(): gram = lax.psum(gram_part, 'mem')  21.7 us
    dot_general x4, matrix products, on_device(): jnp.dot(cross * scale * spread(blocks), w_batch, precision=lax.Precision....  21.4 us
    another operation x4, other arithmetic, on_device(): jax.scipy.linalg.cho_solve((factor, True), innov).astype(jnp.bfloat16)  19.7 us
    dot_general x4, matrix products, on_device(): cross_part = jnp.dot(field, y_batch.T, precision=lax.Precision.HIGHEST)  15.9 us
    unnamed x22, local copies, waits for them, and re-layouts  7.98 us
  transfers between devices with their start and end apart: 8, of which 8 were waited for; matrix products, arithmetic and copies ran while one was open for 0% of the time, Pallas kernels for 0%

commit v1 on v0

--- a/solution.py
+++ b/solution.py
@@ -23,7 +23,7 @@
     num_obs = obs_anom.shape[0]
     arrivals = order.shape[1]
     gram_part = jnp.dot(obs_anom, obs_anom.T, preferred_element_type=jnp.float32)
-    gram = lax.psum(gram_part, "mem")
+    gram = jnp.sum(lax.all_gather(gram_part, "mem"), axis=0)
     spd = gram * scale + jnp.eye(num_obs, dtype=jnp.float32)
     factor = jnp.linalg.cholesky(spd)
     weights_own = jax.scipy.linalg.cho_solve((factor, True), innov).astype(jnp.bfloat16)

time: 314 us -> 294 us (0.936)
  waiting for transfers between devices: 173 us -> 152 us
    psum x1 -> x0, waiting for transfers between devices: 21.7 us -> none  [on_device(): gram = lax.psum(gram_part, 'mem')]
  transfers between devices with their start and end apart: 8 -> 7, of which waited for: 8 -> 7; matrix products, arithmetic and copies ran while one was open for 0% -> 0% of each run, Pallas kernels for 0% -> 0%
where the time goes in v1:
time: 294 us; the launch traced here: 293 us
  waiting for transfers between devices  152 us (52%)
  other arithmetic  56.2 us (19%)
  matrix products  43 us (15%)
  between operations  22.2 us (8%)
  local copies, waits for them, and re-layouts  13.4 us (5%)
  starting transfers between devices  3.51 us (1%)
    ppermute x3, waiting for transfers between devices, from_behind(): return lax.ppermute(value, axis, pairs)  80.8 us
    psum x4, waiting for transfers between devices, on_device(): cross = lax.psum(cross_part, 'mem')  71.4 us
    another operation x6, other arithmetic, on_device(): factor = jnp.linalg.cholesky(spd)  34 us
    dot_general x4, matrix products, on_device(): jnp.dot(cross * scale * spread(blocks), w_batch, precision=lax.Precision....  21.4 us
    another operation x4, other arithmetic, on_device(): jax.scipy.linalg.cho_solve((factor, True), innov).astype(jnp.bfloat16)  19.7 us
    dot_general x4, matrix products, on_device(): cross_part = jnp.dot(field, y_batch.T, precision=lax.Precision.HIGHEST)  15.9 us
    unnamed x22, local copies, waits for them, and re-layouts  7.98 us
  transfers between devices with their start and end apart: 7, of which 7 were waited for; matrix products, arithmetic and copies ran while one was open for 0% of the time, Pallas kernels for 0%

profile of v1, /device:TPU:0, one launch (start us, length us, event | category | flops | bytes accessed | tf_op | source)
XLA Modules:
  0.0 293.0 jit_solution(16287565726024425668)
XLA Ops:
  6.5 1.6 fusion.46
  8.2 2.3 all-gather
  10.5 0.1 copy.13
  10.7 0.1 copy.14
  10.8 0.1 fusion.19
  10.9 11.7 %cholesky.50 = f32[128,128]{1,0:T(8,128)S(1)} custom-call(f32[128,128]{1,0:T(8,128)S(1)} %cholesky.118), custom_call_target="Cholesky" | custom-call | tf_op jit(solution)/shard_map/jit(cholesky)/cholesky | solution.py:28
  22.7 9.8 %custom-call.18 = f32[1,128,128]{1,2,0:T(8,128)S(1)} custom-call(f32[1,128,128]{2,1,0:T(8,128)S(1)} %get-tuple-element.28), custom_call_target="InvertDiagBlocksLowerTriangular" | custom-call | tf_op jit(solution)/shard_map/jit(cholesky)/cholesky | solution.py:28
  32.5 0.2 constant_dynamic-update-slice_fusion
  32.7 0.3 convolution_subtract_fusion.2
  33.0 11.7 %cholesky.105 = f32[128,128]{1,0:T(8,128)S(1)} custom-call(f32[128,128]{1,0:T(8,128)S(1)} %convolution_subtract_fusion.2), custom_call_target="Cholesky" | custom-call | tf_op jit(solution)/shard_map/jit(cholesky)/cholesky | solution.py:28
  44.7 0.7 compare_reduce_fusion
  46.8 0.1 triangular_solve.76
  46.8 4.1 %while.1 = (s32[]{:T(128)}, f32[256,256]{1,0:T(8,128)S(1)}, s32[2,2]{1,0:T(2,128)S(1)}, f32[2,128,128]{2,1,0:T(8,128)S(1)}, s32[]{:T(128)}) while((s32[]{:T(128)}, f32[256,256]{1,0:T(8,128)S(1)}, s32[2,2]{1,0:T(2,128)S(1)}, f32[2,128,128]{2,1,0:T(8,128)S(1)}, s32[]{:T(128)}) %tuple.30), condition=%wide.while_cond, body=%wide.while_body.sunk | while | flops 2 | bytes 131181 | solution.py:29
  47.0 0.6 fusion.61
  47.6 1.3 bitcast_dynamic-update-slice_fusion.2
  48.9 0.6 fusion.61
  49.5 1.3 bitcast_dynamic-update-slice_fusion.2
  50.9 0.0 copy-start.5
  50.9 19.7 %custom-call.19 = f32[2,128,128]{1,2,0:T(8,128)S(1)} custom-call(f32[2,128,128]{2,1,0:T(8,128)S(1)} %get-tuple-element.12), custom_call_target="InvertDiagBlocksLowerTriangular" | custom-call | tf_op jit(solution)/shard_map/jit(_cho_solve)/triangular_solve | solution.py:29
  70.6 0.6 fusion.16
  71.2 0.6 convolution_subtract_fusion.1
  71.8 0.0 copy-start.9
  71.8 0.6 fusion.24
  72.5 0.6 fusion.23
  73.1 0.6 convolution_subtract_fusion
  73.7 0.6 fusion
  74.3 0.2 fusion.43
  74.5 2.9 collective-permute-start
  77.4 27.5 %collective-permute-done = bf16[2,256,1024]{2,1,0:T(8,128)(2,1)S(1)} collective-permute-done((bf16[2,256,1024]{2,1,0:T(8,128)(2,1)S(1)}, bf16[2,256,1024]{2,1,0:T(8,128)(2,1)S(1)}, u32[]{:S(2)}, u32[]{:S(2)}) %collective-permute-start) | collective-permute-done | bytes 1048608 | tf_op jit(solution)/shard_map/ppermute | solution.py:10
  104.9 28.3 %collective-permute-done.1 = bf16[2,256,1024]{2,1,0:T(8,128)(2,1)} collective-permute-done((bf16[2,256,1024]{2,1,0:T(8,128)(2,1)S(1)}, bf16[2,256,1024]{2,1,0:T(8,128)(2,1)}, u32[]{:S(2)}, u32[]{:S(2)}) %collective-permute-start.1) | collective-permute-done | bytes 1048608 | tf_op jit(solution)/shard_map/ppermute | solution.py:10
  133.2 0.7 fusion.45
  135.8 25.1 %collective-permute-done.2 = bf16[2,256,1024]{2,1,0:T(8,128)(2,1)} collective-permute-done((bf16[2,256,1024]{2,1,0:T(8,128)(2,1)}, bf16[2,256,1024]{2,1,0:T(8,128)(2,1)}, u32[]{:S(2)}, u32[]{:S(2)}) %collective-permute-start.2) | collective-permute-done | bytes 1048608 | tf_op jit(solution)/shard_map/ppermute | solution.py:10
  160.9 1.9 pad_maximum_fusion
  162.8 1.9 copy-done.3
  164.8 3.2 %convolution_bitcast_fusion = f32[1024,256]{0,1:T(8,128)} fusion(f32[1024,1024]{1,0:T(8,128)S(1)} %copy-done.4, bf16[4,2,256,1024]{3,2,1,0:T(8,128)(2,1)S(1)} %pad_maximum_fusion, s32[]{:T(128)S(6)} %select_n.23), kind=kOutput, calls=%fused_computation.7 | convolution fusion | flops 3221225472 | bytes 5767172 | tf_op jit(solution)/shard_map/dot_general | solution.py:48
  167.9 0.0 all-reduce.6.cloned.1.call-update
  167.9 0.3 all-reduce.8.cloned.1.call-start
  173.7 0.2 select_reduce_fusion
  174.0 9.4 %all-reduce.6.cloned.1.call-done = f32[1024,256]{0,1:T(8,128)} async-done(((f32[1024,256]{0,1:T(8,128)}), f32[1024,256]{0,1:T(8,128)}) %all-reduce.6.cloned.1.call-update) | async-done | bytes 1048592 | tf_op jit(solution)/shard_map/psum | solution.py:49
  183.4 0.1 broadcast_in_dim.19
  183.5 4.9 %convolution_add_fusion.3 = f32[1024,1024]{1,0:T(8,128)S(1)} fusion(f32[1024,1024]{1,0:T(8,128)} %param.7, f32[32,8,8,128]{3,2,1,0:T(8,128)S(1)} %bitcast.128, f32[1024,256]{0,1:T(8,128)} %all-reduce.6.cloned.1.call-done, bf16[4,2,256,1024]{3,2,1,0:T(8,128)(2,1)} %copy-done.3, s32[]{:T(128)S(6)} %select_n.23, s32[]{:T(128)S(6)} %add.82), kind=kOutput, calls=%fused_computation.6 | convolution fusion | flops 3222798336 | bytes 11010056 | tf_op jit(solution)/shard_map/dot_general | solution.py:50
  188.4 0.0 copy-start.2
  188.4 2.0 copy-done.2
  190.5 4.2 %fusion.11 = f32[1024,256]{0,1:T(8,128)} fusion(f32[1024,1024]{1,0:T(8,128)S(1)} %convolution_add_fusion.3, bf16[4,2,256,1024]{3,2,1,0:T(8,128)(2,1)} %copy-done.3, s32[]{:T(128)S(6)} %select_n.24), kind=kOutput, calls=%fused_computation.34 | convolution fusion | flops 3221225472 | bytes 5767172 | tf_op jit(solution)/shard_map/dot_general | solution.py:48
  194.7 0.0 all-reduce.8.cloned.1.call-update
  194.7 0.0 all-reduce.10.cloned.1.call-start
  194.8 20.7 %all-reduce.8.cloned.1.call-done = f32[1024,256]{0,1:T(8,128)} async-done(((f32[1024,256]{0,1:T(8,128)}), f32[1024,256]{0,1:T(8,128)}) %all-reduce.8.cloned.1.call-update) | async-done | bytes 1048592 | tf_op jit(solution)/shard_map/psum | solution.py:49
  215.5 0.1 broadcast_in_dim.39
  215.6 4.9 %convolution_add_fusion.2 = f32[1024,1024]{1,0:T(8,128)S(1)} fusion(f32[1024,1024]{1,0:T(8,128)} %copy-done.2, f32[32,8,8,128]{3,2,1,0:T(8,128)S(1)} %bitcast.126, f32[1024,256]{0,1:T(8,128)} %all-reduce.8.cloned.1.call-done, bf16[4,2,256,1024]{3,2,1,0:T(8,128)(2,1)} %copy-done.3, s32[]{:T(128)S(6)} %select_n.24, s32[]{:T(128)S(6)} %add.82), kind=kOutput, calls=%fused_computation.5 | convolution fusion | flops 3222798336 | bytes 11010056 | tf_op jit(solution)/shard_map/dot_general | solution.py:50
  220.5 0.0 copy-start.1
  220.5 2.0 copy-done.1
  222.5 4.2 %fusion.10 = f32[1024,256]{0,1:T(8,128)} fusion(f32[1024,1024]{1,0:T(8,128)S(1)} %convolution_add_fusion.2, bf16[4,2,256,1024]{3,2,1,0:T(8,128)(2,1)} %copy-done.3, s32[]{:T(128)S(6)} %select_n.25), kind=kOutput, calls=%fused_computation.31 | convolution fusion | flops 3221225472 | bytes 5767172 | tf_op jit(solution)/shard_map/dot_general | solution.py:48
  226.8 0.0 all-reduce.10.cloned.1.call-update
  226.8 0.3 all-reduce.12.cloned.1.call-start
  227.1 20.4 %all-reduce.10.cloned.1.call-done = f32[1024,256]{0,1:T(8,128)} async-done(((f32[1024,256]{0,1:T(8,128)}), f32[1024,256]{0,1:T(8,128)}) %all-reduce.10.cloned.1.call-update) | async-done | bytes 1048592 | tf_op jit(solution)/shard_map/psum | solution.py:49
  247.6 0.1 broadcast_in_dim.41
  247.7 4.9 %convolution_add_fusion.1 = f32[1024,1024]{1,0:T(8,128)S(1)} fusion(f32[1024,1024]{1,0:T(8,128)} %copy-done.1, f32[32,8,8,128]{3,2,1,0:T(8,128)S(1)} %bitcast.127, f32[1024,256]{0,1:T(8,128)} %all-reduce.10.cloned.1.call-done, bf16[4,2,256,1024]{3,2,1,0:T(8,128)(2,1)} %copy-done.3, s32[]{:T(128)S(6)} %select_n.25, s32[]{:T(128)S(6)} %add.82), kind=kOutput, calls=%fused_computation.4 | convolution fusion | flops 3222798336 | bytes 11010056 | tf_op jit(solution)/shard_map/dot_general | solution.py:50
  252.6 0.0 copy-start
  252.6 2.0 copy-done
  254.6 4.2 %fusion.9 = f32[1024,256]{0,1:T(8,128)} fusion(f32[1024,1024]{1,0:T(8,128)S(1)} %convolution_add_fusion.1, bf16[4,2,256,1024]{3,2,1,0:T(8,128)(2,1)} %copy-done.3, s32[]{:T(128)S(6)} %select_n.26), kind=kOutput, calls=%fused_computation.28 | convolution fusion | flops 3221225472 | bytes 5767172 | tf_op jit(solution)/shard_map/dot_general | solution.py:48
  258.9 0.0 all-reduce.12.cloned.1.call-update
  258.9 20.8 %all-reduce.12.cloned.1.call-done = f32[1024,256]{0,1:T(8,128)} async-done(((f32[1024,256]{0,1:T(8,128)}), f32[1024,256]{0,1:T(8,128)}) %all-reduce.12.cloned.1.call-update) | async-done | bytes 1048592 | tf_op jit(solution)/shard_map/psum | solution.py:49
  279.7 0.1 broadcast_in_dim.43
  279.8 6.7 %convolution_add_fusion = f32[1024,1024]{1,0:T(8,128)} fusion(f32[1024,1024]{1,0:T(8,128)} %copy-done, f32[32,8,8,128]{3,2,1,0:T(8,128)S(1)} %bitcast.125, f32[1024,256]{0,1:T(8,128)} %all-reduce.12.cloned.1.call-done, bf16[4,2,256,1024]{3,2,1,0:T(8,128)(2,1)} %copy-done.3, s32[]{:T(128)S(6)} %select_n.26, s32[]{:T(128)S(6)} %add.82), kind=kOutput, calls=%fused_computation.3 | convolution fusion | flops 3222798336 | bytes 11010056 | tf_op jit(solution)/shard_map/dot_general | solution.py:50
  (30 shorter events, 0.3 us)
Async XLA Ops:
  6.5 64.1 %copy-start.6 = (f32[256,1024]{1,0:T(8,128)S(1)}, f32[256,1024]{1,0:T(8,128)}, u32[]{:S(2)}) copy-start(f32[256,1024]{1,0:T(8,128)} %param.9) | copy-start | bytes 3145732
  6.5 176.9 %all-reduce.6.cloned.1.call-start = ((), (), s32[]{:S(2)}) async-start(), calls=%async_computation | async-start | bytes 2097152 | tf_op jit(solution)/shard_map/psum | solution.py:49
  50.9 23.4 %copy-start.5 = (bf16[256,1024]{1,0:T(8,128)(2,1)S(1)}, bf16[256,1024]{1,0:T(8,128)(2,1)}, u32[]{:S(2)}) copy-start(bf16[256,1024]{1,0:T(8,128)(2,1)} %param.8) | copy-start | bytes 1572868
  71.8 61.4 %copy-start.9 = (s32[1,4]{1,0:T(1,128)S(1)}, s32[1,4]{1,0:T(1,128)}, u32[]{:S(2)}) copy-start(s32[1,4]{1,0:T(1,128)} %param.13) | copy-start | bytes 52
  74.5 30.4 %collective-permute-start = (bf16[2,256,1024]{2,1,0:T(8,128)(2,1)S(1)}, bf16[2,256,1024]{2,1,0:T(8,128)(2,1)S(1)}, u32[]{:S(2)}, u32[]{:S(2)}) collective-permute-start(bf16[2,256,1024]{2,1,0:T(8,128)(2,1)S(1)} %get-tuple-element.24), channel_id=1, source_target_pairs={{0,2},{2,4},{4,6},{6,8},{8,10},{10,12},{12,14},{14,16},{16,18},{18... | collective-permute-start | bytes 3145736 | tf_op jit(solution)/shard_map/ppermute | solution.py:10
  104.9 28.3 %collective-permute-start.1 = (bf16[2,256,1024]{2,1,0:T(8,128)(2,1)S(1)}, bf16[2,256,1024]{2,1,0:T(8,128)(2,1)}, u32[]{:S(2)}, u32[]{:S(2)}) collective-permute-start(bf16[2,256,1024]{2,1,0:T(8,128)(2,1)S(1)} %collective-permute-done), channel_id=1, source_target_pairs={{0,2},{2,4},{4,6},{6,8},{8,10},{10,12},{12,14},{14,16},{16,18},{18... | collective-permute-start | bytes 3145736 | tf_op jit(solution)/shard_map/ppermute | solution.py:10
  133.2 27.7 %collective-permute-start.2 = (bf16[2,256,1024]{2,1,0:T(8,128)(2,1)}, bf16[2,256,1024]{2,1,0:T(8,128)(2,1)}, u32[]{:S(2)}, u32[]{:S(2)}) collective-permute-start(bf16[2,256,1024]{2,1,0:T(8,128)(2,1)} %collective-permute-done.1), channel_id=1, source_target_pairs={{0,2},{2,4},{4,6},{6,8},{8,10},{10,12},{12,14},{14,16},{16,18},{18... | collective-permute-start | bytes 3145736 | tf_op jit(solution)/shard_map/ppermute | solution.py:10
  160.9 3.9 %copy-start.4 = (f32[1024,1024]{1,0:T(8,128)S(1)}, f32[1024,1024]{1,0:T(8,128)}, u32[]{:S(2)}) copy-start(f32[1024,1024]{1,0:T(8,128)} %param.7) | copy-start | bytes 12582916
  162.8 1.9 copy-start.3
  164.7 9.0 %copy-start.8 = (s32[1,4,8,4]{2,3,1,0:T(4,128)S(1)}, s32[1,4,8,4]{2,3,1,0:T(4,128)}, u32[]{:S(2)}) copy-start(s32[1,4,8,4]{2,3,1,0:T(4,128)} %param.11) | copy-start | bytes 1540
  164.7 9.0 %copy-start.10 = (f32[8]{0:T(128)S(1)}, f32[8]{0:T(128)}, u32[]{:S(2)}) copy-start(f32[8]{0:T(128)} %param.12) | copy-start | bytes 100
  164.7 9.2 %copy-start.7 = (s32[1,4,8,4]{2,3,1,0:T(4,128)S(1)}, s32[1,4,8,4]{2,3,1,0:T(4,128)}, u32[]{:S(2)}) copy-start(s32[1,4,8,4]{2,3,1,0:T(4,128)} %param.10) | copy-start | bytes 1540
  167.9 47.5 %all-reduce.8.cloned.1.call-start = ((), (), s32[]{:S(2)}) async-start(), calls=%async_computation.1 | async-start | bytes 2097152 | tf_op jit(solution)/shard_map/psum | solution.py:49
  188.4 2.0 copy-start.2
  194.7 52.8 %all-reduce.10.cloned.1.call-start = ((), (), s32[]{:S(2)}) async-start(), calls=%async_computation.2 | async-start | bytes 2097152 | tf_op jit(solution)/shard_map/psum | solution.py:49
  220.5 2.0 copy-start.1
  226.8 52.8 %all-reduce.12.cloned.1.call-start = ((), (), s32[]{:S(2)}) async-start(), calls=%async_computation.3 | async-start | bytes 2097152 | tf_op jit(solution)/shard_map/psum | solution.py:49
  252.6 2.0 copy-start
Sparse Core Ops, SparseCore 0:
  168.1 15.2 all-reduce.5
  194.8 20.5 all-reduce.7
  226.9 20.5 all-reduce.9
  259.0 20.5 all-reduce.11
